TPU v7x, 32 devices: a whole 2x2x4 slice. The times are simulated.
32 devices in a mesh: dp: 4 (over x, core), fsdp: 8 (over z, y).
Axes of the slice: x: 2, y: 2, z: 4, core: 2. Of those that a mesh axis runs over, the one named last changes fastest.
Arguments:
- hidden: bfloat16 [32, 128, 768], P(('dp', 'fsdp')), may hold values from -6 to 6
- sections: int32 [32], P(('dp', 'fsdp')), may hold values from 0 to 3
- lengths: int32 [32], P(('dp', 'fsdp')), may hold values from 32 to 128, as said below
- token_mask: int32 [32, 128], P(('dp', 'fsdp')), may hold values 0 or 1
- cotangent: bfloat16 [32, 128, 768], P(('dp', 'fsdp')), may hold values from -6 to 6
- ln1_gain: bfloat16 [768], P(('dp', 'fsdp')), may hold values from 0.5 to 1.5
- ln1_bias: bfloat16 [768], P(('dp', 'fsdp')), may hold values from -1.5 to 1.5
- qkv_weight: bfloat16 [768, 2304], P(('dp', 'fsdp')), may hold values from -0.21875 to 0.21875
- qv_bias: bfloat16 [1536], P(('dp', 'fsdp')), may hold values from -1.5 to 1.5
- out_weight: bfloat16 [768, 768], P(('dp', 'fsdp')), may hold values from -0.875 to 0.875
- out_bias: bfloat16 [768], P(('dp', 'fsdp')), may hold values from -1.5 to 1.5
- ln2_gain: bfloat16 [768], P(('dp', 'fsdp')), may hold values from 0.5 to 1.5
- ln2_bias: bfloat16 [768], P(('dp', 'fsdp')), may hold values from -1.5 to 1.5
- fc_weight: bfloat16 [768, 3072], P(('dp', 'fsdp')), may hold values from -0.21875 to 0.21875
- fc_bias: bfloat16 [3072], P(('dp', 'fsdp')), may hold values from -1.5 to 1.5
- proj_weight: bfloat16 [3072, 768], P(('dp', 'fsdp')), may hold values from -0.109375 to 0.109375
- proj_bias: bfloat16 [768], P(('dp', 'fsdp')), may hold values from -1.5 to 1.5
Outputs:
- hidden_out: bfloat16 [32, 128, 768], P(('dp', 'fsdp'))
- grad_hidden: float32 [32, 128, 768], P(('dp', 'fsdp'))
- grad_ln1_gain: float32 [768], P(('dp', 'fsdp'))
- grad_ln1_bias: float32 [768], P(('dp', 'fsdp'))
- grad_qkv_weight: float32 [768, 2304], P(('dp', 'fsdp'))
- grad_qv_bias: float32 [1536], P(('dp', 'fsdp'))
- grad_out_weight: float32 [768, 768], P(('dp', 'fsdp'))
- grad_out_bias: float32 [768], P(('dp', 'fsdp'))
- grad_ln2_gain: float32 [768], P(('dp', 'fsdp'))
- grad_ln2_bias: float32 [768], P(('dp', 'fsdp'))
- grad_fc_weight: float32 [768, 3072], P(('dp', 'fsdp'))
- grad_fc_bias: float32 [3072], P(('dp', 'fsdp'))
- grad_proj_weight: float32 [3072, 768], P(('dp', 'fsdp'))
- grad_proj_bias: float32 [768], P(('dp', 'fsdp'))
Inputs may be any that keep to these rules, and one draw needn't show every extreme that they name: `lengths`: some sequence has exactly 128 valid tokens and some has exactly 32.
All inputs are finite; a program needn't handle non-finite values. No bound on the sum of `token_mask` on one device may be relied on, other than what follows from the above.
Results may differ from a plain program's by a relative error of at most 0.013.
Values may be sent and summed in bfloat16 or wider, within the bound.
A program may use at most 192 MiB of HBM per device.

v0:
```python
import jax
import jax.numpy as jnp
from jax import lax
from jax.sharding import PartitionSpec as P

HEAD_DIM = 64
PASSES = 4
epsilon = 1e-05
score_scale = 0.125
gelu_coef = 0.7978845608028654


def layer_norm(values, gain, shift):
    centre = values - jnp.mean(values, axis=-1, keepdims=True)
    spread = jnp.mean(centre * centre, axis=-1, keepdims=True)
    return centre * lax.rsqrt(spread + epsilon) * gain + shift


def gelu_tanh(values):
    return (
        0.5 * values * (1.0 + jnp.tanh(gelu_coef * (values + 0.044715 * values * values * values)))
    )


def fetch_attention(ln1_gain, ln1_bias, qkv_weight, qv_bias, out_weight, out_bias):
    return (
        lax.all_gather(ln1_gain, ("dp", "fsdp"), axis=0, tiled=True),
        lax.all_gather(ln1_bias, ("dp", "fsdp"), axis=0, tiled=True),
        lax.all_gather(qkv_weight, ("dp", "fsdp"), axis=0, tiled=True),
        lax.all_gather(qv_bias, ("dp", "fsdp"), axis=0, tiled=True),
        lax.all_gather(out_weight, ("dp", "fsdp"), axis=0, tiled=True),
        lax.all_gather(out_bias, ("dp", "fsdp"), axis=0, tiled=True),
    )


def fetch_mlp(ln2_gain, ln2_bias, fc_weight, fc_bias, proj_weight, proj_bias):
    return (
        lax.all_gather(ln2_gain, ("dp", "fsdp"), axis=0, tiled=True),
        lax.all_gather(ln2_bias, ("dp", "fsdp"), axis=0, tiled=True),
        lax.all_gather(fc_weight, ("dp", "fsdp"), axis=0, tiled=True),
        lax.all_gather(fc_bias, ("dp", "fsdp"), axis=0, tiled=True),
        lax.all_gather(proj_weight, ("dp", "fsdp"), axis=0, tiled=True),
        lax.all_gather(proj_bias, ("dp", "fsdp"), axis=0, tiled=True),
    )


def allowed_rows(key_valid, block_rows, seq_len):
    query_pos = jnp.arange(block_rows, dtype=jnp.int32)[:, None]
    key_pos = jnp.arange(seq_len, dtype=jnp.int32)[None, :]
    return (key_pos <= query_pos) & (key_valid[:, None, :] | (key_pos == query_pos))


def attend_forward(queries, key_rows, values, key_valid):
    seq_len = queries.shape[1]
    block_rows = min(512, seq_len)
    scores = (
        jnp.einsum("gqhd,gkhd->ghqk", queries, key_rows, preferred_element_type=jnp.float32)
        * score_scale
    )
    allowed = allowed_rows(key_valid, block_rows, seq_len)[:, None]
    scores = jnp.where(allowed, scores, -1e30)
    row_max = jnp.max(scores, axis=-1, keepdims=True)
    expo = jnp.exp(scores - row_max)
    row_total = jnp.sum(expo, axis=-1, keepdims=True)
    probs = (expo / row_total).astype(jnp.bfloat16)
    outputs = jnp.einsum("ghqk,gkhd->gqhd", probs, values, preferred_element_type=jnp.float32)
    totals = (row_max + jnp.log(row_total))[..., 0]
    return (outputs, totals)


def attend_backward(queries, key_rows, values, log_totals, grad_mixed, key_valid):
    seq_len = queries.shape[1]
    block_rows = min(512, seq_len)
    scores = (
        jnp.einsum("gqhd,gkhd->ghqk", queries, key_rows, preferred_element_type=jnp.float32)
        * score_scale
    )
    allowed = allowed_rows(key_valid, block_rows, seq_len)[:, None]
    block_totals = log_totals[:, :, 0:block_rows, None]
    probs = jnp.where(allowed, jnp.exp(scores - block_totals), 0.0)
    probs_low = probs.astype(jnp.bfloat16)
    grad_values = jnp.einsum(
        "ghqk,gqhd->gkhd", probs_low, grad_mixed, preferred_element_type=jnp.float32
    )
    grad_probs = jnp.einsum(
        "gqhd,gkhd->ghqk", grad_mixed, values, preferred_element_type=jnp.float32
    )
    inner = jnp.sum(grad_probs * probs, axis=-1, keepdims=True)
    grad_scores = (probs * (grad_probs - inner)).astype(jnp.bfloat16)
    grad_queries = (
        jnp.einsum("ghqk,gkhd->gqhd", grad_scores, key_rows, preferred_element_type=jnp.float32)
        * score_scale
    )
    grad_keys = (
        jnp.einsum("ghqk,gqhd->gkhd", grad_scores, queries, preferred_element_type=jnp.float32)
        * score_scale
    )
    return (grad_queries, grad_keys, grad_values)


def forward_pass(state, weights, key_valid, live, seq_count, seq_len):
    (gain_one, shift_one, qkv_w, qv_b, out_w, out_b), (
        gain_two,
        shift_two,
        fc_w,
        fc_b,
        proj_w,
        proj_b,
    ) = weights
    row_count, model_width = state.shape
    head_count = model_width // HEAD_DIM
    normed = layer_norm(state, gain_one.astype(jnp.float32), shift_one.astype(jnp.float32)).astype(
        jnp.bfloat16
    )
    qv_float = qv_b.astype(jnp.float32)
    bias_full = jnp.concatenate(
        [qv_float[:model_width], jnp.zeros((model_width,), jnp.float32), qv_float[model_width:]]
    )
    joined = (jnp.dot(normed, qkv_w, preferred_element_type=jnp.float32) + bias_full).astype(
        jnp.bfloat16
    )
    split = joined.reshape(seq_count, seq_len, 3, head_count, HEAD_DIM)
    queries = split[:, :, 0]
    key_rows = split[:, :, 1]
    values = split[:, :, 2]
    mixed_float, log_totals = attend_forward(queries, key_rows, values, key_valid)
    mixed = mixed_float.reshape(row_count, model_width).astype(jnp.bfloat16)
    middle = (
        state
        + jnp.dot(mixed, out_w, preferred_element_type=jnp.float32)
        + out_b.astype(jnp.float32)
    )
    normed_two = layer_norm(
        middle, gain_two.astype(jnp.float32), shift_two.astype(jnp.float32)
    ).astype(jnp.bfloat16)
    upper = jnp.dot(normed_two, fc_w, preferred_element_type=jnp.float32) + fc_b.astype(jnp.float32)
    activated = gelu_tanh(upper).astype(jnp.bfloat16)
    result = (
        middle
        + jnp.dot(activated, proj_w, preferred_element_type=jnp.float32)
        + proj_b.astype(jnp.float32)
    )
    record = (
        state,
        normed,
        queries,
        key_rows,
        values,
        log_totals,
        mixed,
        middle,
        normed_two,
        upper,
        activated,
    )
    return (jnp.where(live, result, state), record)


def backward_mlp(grad_next, record, weights, live):
    (
        state,
        normed,
        queries,
        key_rows,
        values,
        log_totals,
        mixed,
        middle,
        normed_two,
        upper,
        activated,
    ) = record
    (gain_one, shift_one, qkv_w, qv_b, out_w, out_b), (
        gain_two,
        shift_two,
        fc_w,
        fc_b,
        proj_w,
        proj_b,
    ) = weights
    grad_out = jnp.where(live, grad_next, 0.0)
    grad_branch = grad_out.astype(jnp.bfloat16)
    term_proj_b = jnp.sum(grad_branch.astype(jnp.float32), axis=0)
    term_proj_w = jnp.einsum(
        "ti,to->io", activated, grad_branch, preferred_element_type=jnp.float32
    )
    grad_act = jnp.einsum("to,io->ti", grad_branch, proj_w, preferred_element_type=jnp.float32)
    gelu_pull = jax.vjp(gelu_tanh, upper)[1]
    grad_upper = gelu_pull(grad_act)[0].astype(jnp.bfloat16)
    term_fc_b = jnp.sum(grad_upper.astype(jnp.float32), axis=0)
    term_fc_w = jnp.einsum("td,tf->df", normed_two, grad_upper, preferred_element_type=jnp.float32)
    grad_normed_two = jnp.einsum("tf,df->td", grad_upper, fc_w, preferred_element_type=jnp.float32)
    norm_pull_two = jax.vjp(
        layer_norm, middle, gain_two.astype(jnp.float32), shift_two.astype(jnp.float32)
    )[1]
    grad_mid_norm, term_gain_two, term_shift_two = norm_pull_two(grad_normed_two)
    grad_middle = grad_out + grad_mid_norm
    mlp_terms = (term_gain_two, term_shift_two, term_fc_w, term_fc_b, term_proj_w, term_proj_b)
    return (grad_middle, mlp_terms)


def backward_attention(grad_next, grad_middle, record, weights, key_valid, live):
    (
        state,
        normed,
        queries,
        key_rows,
        values,
        log_totals,
        mixed,
        middle,
        normed_two,
        upper,
        activated,
    ) = record
    (gain_one, shift_one, qkv_w, qv_b, out_w, out_b), mlp_weights = weights
    row_count, model_width = state.shape
    grad_attn = grad_middle.astype(jnp.bfloat16)
    term_out_b = jnp.sum(grad_attn.astype(jnp.float32), axis=0)
    term_out_w = jnp.einsum("td,te->de", mixed, grad_attn, preferred_element_type=jnp.float32)
    grad_mixed = jnp.einsum(
        "te,de->td", grad_attn, out_w, preferred_element_type=jnp.float32
    ).astype(jnp.bfloat16)
    grad_mixed = grad_mixed.reshape(queries.shape)
    grad_queries, grad_keys, grad_values = attend_backward(
        queries, key_rows, values, log_totals, grad_mixed, key_valid
    )
    grad_joined = (
        jnp.stack([grad_queries, grad_keys, grad_values], axis=2)
        .reshape(row_count, 3 * model_width)
        .astype(jnp.bfloat16)
    )
    column_sums = jnp.sum(grad_joined.astype(jnp.float32), axis=0)
    term_qv_b = jnp.concatenate([column_sums[:model_width], column_sums[2 * model_width :]])
    term_qkv_w = jnp.einsum("td,tk->dk", normed, grad_joined, preferred_element_type=jnp.float32)
    grad_normed = jnp.einsum("tk,dk->td", grad_joined, qkv_w, preferred_element_type=jnp.float32)
    norm_pull_one = jax.vjp(
        layer_norm, state, gain_one.astype(jnp.float32), shift_one.astype(jnp.float32)
    )[1]
    grad_state_norm, term_gain_one, term_shift_one = norm_pull_one(grad_normed)
    grad_prev = grad_middle + grad_state_norm + jnp.where(live, 0.0, grad_next)
    attention_terms = (term_gain_one, term_shift_one, term_qkv_w, term_qv_b, term_out_w, term_out_b)
    return (grad_prev, attention_terms)


def body(
    hidden,
    sections,
    lengths,
    token_mask,
    cotangent,
    ln1_gain,
    ln1_bias,
    qkv_weight,
    qv_bias,
    out_weight,
    out_bias,
    ln2_gain,
    ln2_bias,
    fc_weight,
    fc_bias,
    proj_weight,
    proj_bias,
):
    seq_count, seq_len, model_width = hidden.shape
    row_count = seq_count * seq_len
    key_pos = jnp.arange(seq_len, dtype=jnp.int32)
    key_valid = (key_pos[None, :] < lengths[:, None]) & (token_mask == 1)

    def gather_both():
        return (
            fetch_attention(ln1_gain, ln1_bias, qkv_weight, qv_bias, out_weight, out_bias),
            fetch_mlp(ln2_gain, ln2_bias, fc_weight, fc_bias, proj_weight, proj_bias),
        )

    state = hidden.reshape(row_count, model_width).astype(jnp.float32)
    records = []
    for section_index in range(PASSES):
        current = gather_both()
        live = jnp.repeat(sections >= section_index, seq_len)[:, None]
        state, record = forward_pass(state, current, key_valid, live, seq_count, seq_len)
        records.append(record)
    hidden_out = state.astype(jnp.bfloat16).reshape(seq_count, seq_len, model_width)
    grad_state = cotangent.reshape(row_count, model_width).astype(jnp.float32)
    attention_sum = None
    mlp_sum = None
    for section_index in reversed(range(PASSES)):
        current = gather_both()
        live = jnp.repeat(sections >= section_index, seq_len)[:, None]
        grad_middle, mlp_terms = backward_mlp(grad_state, records[section_index], current, live)
        if mlp_sum is None:
            mlp_sum = mlp_terms
        else:
            mlp_sum = jax.tree.map(jnp.add, mlp_sum, mlp_terms)
        grad_state, attention_terms = backward_attention(
            grad_state, grad_middle, records[section_index], current, key_valid, live
        )
        if attention_sum is None:
            attention_sum = attention_terms
        else:
            attention_sum = jax.tree.map(jnp.add, attention_sum, attention_terms)
    sum_gain_one, sum_shift_one, sum_qkv_w, sum_qv_b, sum_out_w, sum_out_b = attention_sum
    attention_grads = (
        lax.psum_scatter(sum_gain_one, ("dp", "fsdp"), scatter_dimension=0, tiled=True),
        lax.psum_scatter(sum_shift_one, ("dp", "fsdp"), scatter_dimension=0, tiled=True),
        lax.psum_scatter(sum_qkv_w, ("dp", "fsdp"), scatter_dimension=0, tiled=True),
        lax.psum_scatter(sum_qv_b, ("dp", "fsdp"), scatter_dimension=0, tiled=True),
        lax.psum_scatter(sum_out_w, ("dp", "fsdp"), scatter_dimension=0, tiled=True),
        lax.psum_scatter(sum_out_b, ("dp", "fsdp"), scatter_dimension=0, tiled=True),
    )
    sum_gain_two, sum_shift_two, sum_fc_w, sum_fc_b, sum_proj_w, sum_proj_b = mlp_sum
    finished = (
        lax.psum_scatter(sum_gain_two, ("dp", "fsdp"), scatter_dimension=0, tiled=True),
        lax.psum_scatter(sum_shift_two, ("dp", "fsdp"), scatter_dimension=0, tiled=True),
        lax.psum_scatter(sum_fc_w, ("dp", "fsdp"), scatter_dimension=0, tiled=True),
        lax.psum_scatter(sum_fc_b, ("dp", "fsdp"), scatter_dimension=0, tiled=True),
        lax.psum_scatter(sum_proj_w, ("dp", "fsdp"), scatter_dimension=0, tiled=True),
        lax.psum_scatter(sum_proj_b, ("dp", "fsdp"), scatter_dimension=0, tiled=True),
    )
    grad_hidden = grad_state.reshape(seq_count, seq_len, model_width)
    return (
        hidden_out,
        grad_hidden,
        attention_grads[0],
        attention_grads[1],
        attention_grads[2],
        attention_grads[3],
        attention_grads[4],
        attention_grads[5],
        finished[0],
        finished[1],
        finished[2],
        finished[3],
        finished[4],
        finished[5],
    )


def solution(mesh):
    return jax.shard_map(
        body,
        mesh=mesh,
        in_specs=(
            P(("dp", "fsdp"), None, None),
            P(("dp", "fsdp")),
            P(("dp", "fsdp")),
            P(("dp", "fsdp"), None),
            P(("dp", "fsdp"), None, None),
            P(("dp", "fsdp")),
            P(("dp", "fsdp")),
            P(("dp", "fsdp"), None),
            P(("dp", "fsdp")),
            P(("dp", "fsdp"), None),
            P(("dp", "fsdp")),
            P(("dp", "fsdp")),
            P(("dp", "fsdp")),
            P(("dp", "fsdp"), None),
            P(("dp", "fsdp")),
            P(("dp", "fsdp"), None),
            P(("dp", "fsdp")),
        ),
        out_specs=(
            P(("dp", "fsdp"), None, None),
            P(("dp", "fsdp"), None, None),
            P(("dp", "fsdp")),
            P(("dp", "fsdp")),
            P(("dp", "fsdp"), None),
            P(("dp", "fsdp")),
            P(("dp", "fsdp"), None),
            P(("dp", "fsdp")),
            P(("dp", "fsdp")),
            P(("dp", "fsdp")),
            P(("dp", "fsdp"), None),
            P(("dp", "fsdp")),
            P(("dp", "fsdp"), None),
            P(("dp", "fsdp")),
        ),
        check_vma=False,
    )
```

profile of v0, /device:TPU:0, one launch (start us, length us, event | category | flops | bytes accessed | tf_op | source)
XLA Modules:
  0.0 899.9 jit_solution(807125739731733085)
XLA Ops:
  18.1 43.0 %all-reduce.17 = (bf16[1536]{0:T(1024)(128)(2,1)S(1)}, bf16[768]{0:T(1024)(128)(2,1)S(1)}, bf16[768]{0:T(1024)(128)(2,1)S(1)}, bf16[768]{0:T(1024)(128)(2,1)S(1)...) all-reduce(bf16[1536]{0:T(1024)(128)(2,1)S(1)} %dynamic-update-slic, ...), channel_id=1, replica_groups=mesh['dp'=4,'fsdp'=8] {'dp','fsdp'}, use_global_device_ids=true, to_apply=%add.2 | all-reduce | flops 9216 | bytes 36864
  64.7 9.0 %all-gather.5.cloned.1.call-done = bf16[768,2304]{1,0:T(8,128)(2,1)} async-done(((bf16[24,2304]{1,0:T(8,128)(2,1)}), bf16[768,2304]{1,0:T(8,128)(2,1)}) %all-gather.5.cloned.1.call-update) | async-done | bytes 3538960 | tf_op jit(solution)/shard_map/all_gather | solution.py:29
  73.8 2.8 fusion
  78.5 51.2 %all-gather.7.cloned.1.call-done = bf16[768,768]{1,0:T(8,128)(2,1)} async-done(((bf16[24,768]{1,0:T(8,128)(2,1)}), bf16[768,768]{1,0:T(8,128)(2,1)}) %all-gather.7.cloned.1.call-update) | async-done | bytes 1179664 | tf_op jit(solution)/shard_map/all_gather | solution.py:31
  129.7 1.7 fusion.176
  132.3 62.8 %all-gather.9.cloned.1.call-done = bf16[768,3072]{1,0:T(8,128)(2,1)} async-done(((bf16[24,3072]{1,0:T(8,128)(2,1)}), bf16[768,3072]{1,0:T(8,128)(2,1)}) %all-gather.9.cloned.1.call-update) | async-done | bytes 4718608 | tf_op jit(solution)/shard_map/all_gather | solution.py:40
  195.1 3.2 convolution_add_fusion.7
  198.3 61.4 %all-gather.11.cloned.1.call-done = bf16[3072,768]{1,0:T(8,128)(2,1)} async-done(((bf16[96,768]{1,0:T(8,128)(2,1)}), bf16[3072,768]{1,0:T(8,128)(2,1)}) %all-gather.11.cloned.1.call-update) | async-done | bytes 4718608 | tf_op jit(solution)/shard_map/all_gather | solution.py:42
  259.7 3.6 fusion.177
  266.2 1.6 copy-done.2
  269.6 4.1 fusion.179
  274.9 1.5 fusion.2
  276.5 2.1 copy.95
  280.8 1.4 convolution_convert_fusion.5
  283.0 3.2 convolution_add_fusion.5
  286.3 4.3 fusion.181
  291.9 1.5 fusion.3
  293.4 2.1 copy.97
  297.7 1.4 convolution_convert_fusion.4
  299.9 3.3 convolution_add_fusion.4
  303.3 5.8 convert_reduce_fusion.3
  309.2 2.3 multiply_reduce_fusion.7
  315.2 1.7 copy.99
  316.9 1.6 convolution_bitcast_fusion.3
  318.6 1.4 multiply_reduce_fusion.3
  321.9 2.0 multiply_reduce_fusion.10
  325.3 5.8 convert_reduce_fusion.2
  331.2 2.5 multiply_reduce_fusion.6
  336.7 1.7 copy.103
  338.4 1.6 convolution_bitcast_fusion.2
  340.0 1.4 multiply_reduce_fusion.2
  343.4 2.0 multiply_reduce_fusion.9
  347.0 3.0 convert_reduce_fusion.1
  350.1 2.3 multiply_reduce_fusion.5
  355.3 1.7 copy.107
  357.0 1.6 convolution_bitcast_fusion.1
  358.7 1.4 multiply_reduce_fusion.1
  361.2 1.9 fusion.185
  363.1 1.9 fusion.184
  365.0 1.9 fusion.183
  368.0 2.0 multiply_reduce_fusion.8
  371.6 3.0 convert_reduce_fusion
  374.6 2.3 multiply_reduce_fusion.4
  379.9 1.7 copy.111
  381.6 5.2 add_add_fusion.3
  386.9 1.8 multiply_reduce_fusion
  390.0 1.7 convert_reduce_fusion.4
  395.6 5.2 add_add_fusion.2
  401.2 6.7 fusion.153
  407.9 5.3 fusion.154
  413.2 1.6 fusion.118
  414.7 11.7 %add_add_fusion = f32[3072,768]{1,0:T(8,128)} fusion(f32[3072,768]{1,0:T(8,128)} %fusion.153, f32[3072,768]{1,0:T(8,128)S(1)} %fusion.118, f32[3072,768]{1,0:T(8,128)} %fusion.154, bf16[128,768]{1,0:T(8,128)(2,1)} %copy-done.123, f32[128,3072]{1,0:T(8,128)S(1)} %copy-done.53), kind=kOutput, calls=%fused_computation | convolution fusion | flops 614596608 | bytes 39518208 | tf_op jit(solution)/shard_map/ti,to->io/dot_general | solution.py:184
  427.1 2.8 fusion.148
  430.1 5.2 fusion.150
  435.3 5.1 fusion.152
  440.4 12.2 %add_add_fusion.1 = f32[768,3072]{1,0:T(8,128)} fusion(f32[768,3072]{1,0:T(8,128)S(1)} %fusion.148, f32[768,3072]{1,0:T(8,128)} %fusion.152, f32[768,3072]{1,0:T(8,128)} %fusion.150, bf16[128,3072]{1,0:T(8,128)(2,1)S(1)} %copy-done.79, f32[128,768]{1,0:T(8,128)S(1)} %copy-done.31, f32[768]{0:T(1024)S(1)} %copy-done.115, f32[768]{0:T(1024)S(1)} %copy-done.94, ...), kind=kOutput, calls=%fused_computation.1 | convolution fusion | flops 611549184 | bytes 38935552 | tf_op jit(solution)/shard_map/td,tf->df/dot_general | solution.py:191
  453.9 1.4 slice.111
  467.0 2.5 fusion.155
  470.6 40.0 %all-reduce.16 = (f32[768]{0:T(1024)S(1)}, f32[768]{0:T(1024)S(1)}, f32[1536]{0:T(1024)S(1)}, f32[768]{0:T(1024)S(1)}, f32[768]{0:T(1024)S(1)}, /*index=5*/f32[7...) all-reduce(f32[768]{0:T(1024)S(1)} %get-tuple-element.154, ...), channel_id=2, replica_groups=mesh['dp'=4,'fsdp'=8] {'dp','fsdp'}, use_global_device_ids=true, to_apply=%region_48.49.clone | all-reduce | flops 9216 | bytes 73728
  515.3 2.4 add_bitcast_fusion
  517.7 4.2 fusion.49
  521.9 87.8 %reduce-scatter.5.cloned.1.call-done = f32[24,2304]{1,0:T(8,128)} async-done(((f32[768,2304]{1,0:T(8,128)}), f32[24,2304]{1,0:T(8,128)}) %reduce-scatter.5.cloned.1.call-update) | async-done | bytes 221200 | tf_op jit(solution)/shard_map/reduce_scatter | solution.py:306
  609.7 141.6 %reduce-scatter.11.cloned.1.call-done = f32[96,768]{1,0:T(8,128)} async-done(((f32[3072,768]{1,0:T(8,128)}), f32[96,768]{1,0:T(8,128)}) %reduce-scatter.11.cloned.1.call-update) | async-done | bytes 294928 | tf_op jit(solution)/shard_map/reduce_scatter | solution.py:317
  751.3 141.6 %reduce-scatter.9.cloned.1.call-done = f32[24,3072]{1,0:T(8,128)} async-done(((f32[768,3072]{1,0:T(8,128)}), f32[24,3072]{1,0:T(8,128)}) %reduce-scatter.9.cloned.1.call-update) | async-done | bytes 294928 | tf_op jit(solution)/shard_map/reduce_scatter | solution.py:315
  (678 shorter events, 75.1 us)
Async XLA Ops:
  7.2 66.6 %all-gather.5.cloned.1.call-start = ((), (), s32[]{:S(2)}) async-start(), calls=%async_computation.4 | async-start | bytes 3649536 | tf_op jit(solution)/shard_map/all_gather | solution.py:29
  7.9 121.8 %all-gather.7.cloned.1.call-start = ((), (), s32[]{:S(2)}) async-start(), calls=%async_computation.5 | async-start | bytes 1216512 | tf_op jit(solution)/shard_map/all_gather | solution.py:31
  8.7 186.4 %all-gather.9.cloned.1.call-start = ((), (), s32[]{:S(2)}) async-start(), calls=%async_computation.6 | async-start | bytes 4866048 | tf_op jit(solution)/shard_map/all_gather | solution.py:40
  9.4 250.3 %all-gather.11.cloned.1.call-start = ((), (), s32[]{:S(2)}) async-start(), calls=%async_computation.7 | async-start | bytes 4866048 | tf_op jit(solution)/shard_map/all_gather | solution.py:42
  10.0 511.9 %reduce-scatter.7.cloned.1.call-start = ((), (), s32[]{:S(2)}) async-start(), calls=%async_computation.9 | async-start | bytes 2433024 | tf_op jit(solution)/shard_map/reduce_scatter | solution.py:308
  61.0 202.5 %copy-start.80 = (f32[768]{0:T(1024)}, f32[768]{0:T(1024)S(1)}, u32[]{:S(2)}) copy-start(f32[768]{0:T(1024)S(1)} %convert_element_type.407) | copy-start | bytes 9220
  61.1 207.4 %copy-start.88 = (f32[768]{0:T(1024)}, f32[768]{0:T(1024)S(1)}, u32[]{:S(2)}) copy-start(f32[768]{0:T(1024)S(1)} %convert_element_type.418) | copy-start | bytes 9220
  61.1 202.5 %copy-start.116 = (f32[768]{0:T(1024)}, f32[768]{0:T(1024)S(1)}, u32[]{:S(2)}) copy-start(f32[768]{0:T(1024)S(1)} %convert_element_type.408) | copy-start | bytes 9220
  61.1 207.4 %copy-start.112 = (f32[768]{0:T(1024)}, f32[768]{0:T(1024)S(1)}, u32[]{:S(2)}) copy-start(f32[768]{0:T(1024)S(1)} %convert_element_type.419) | copy-start | bytes 9220
  61.1 205.0 %copy-start.141 = (f32[768]{0:T(1024)}, f32[768]{0:T(1024)S(1)}, u32[]{:S(2)}) copy-start(f32[768]{0:T(1024)S(1)} %convert_element_type.417) | copy-start | bytes 9220
  61.7 206.8 %copy-start.131 = (f32[3072]{0:T(1024)}, f32[3072]{0:T(1024)S(1)}, u32[]{:S(2)}) copy-start(f32[3072]{0:T(1024)S(1)} %convert_element_type.421) | copy-start | bytes 36868
  61.8 201.8 %copy-start.134 = (f32[2304]{0:T(1024)}, f32[2304]{0:T(1024)S(1)}, u32[]{:S(2)}) copy-start(f32[2304]{0:T(1024)S(1)} %pad_maximum_fusion) | copy-start | bytes 27652
  62.8 13.7 %copy-start.161 = (f32[128]{0:T(128)}, f32[128]{0:T(128)S(1)}, u32[]{:S(2)}) copy-start(f32[128]{0:T(128)S(1)} %broadcast_multiply_fusion.7) | copy-start | bytes 1540
  64.0 12.6 %copy-start.226 = (f32[128]{0:T(128)}, f32[128]{0:T(128)S(1)}, u32[]{:S(2)}) copy-start(f32[128]{0:T(128)S(1)} %fusion.77) | copy-start | bytes 1540
  64.0 12.6 %copy-start.212 = (f32[128]{0:T(128)}, f32[128]{0:T(128)S(1)}, u32[]{:S(2)}) copy-start(f32[128]{0:T(128)S(1)} %fusion.128) | copy-start | bytes 1540
  78.2 51.5 %copy-start.32 = (bf16[1,128,768]{2,1,0:T(8,128)(2,1)S(1)}, bf16[1,128,768]{2,1,0:T(8,128)(2,1)}, u32[]{:S(2)}) copy-start(bf16[1,128,768]{2,1,0:T(8,128)(2,1)} %param.17) | copy-start | bytes 589828
  78.5 119.8 %copy-start.124 = (bf16[12,64,128]{2,1,0:T(8,128)(2,1)}, bf16[12,64,128]{2,1,0:T(8,128)(2,1)S(1)}, u32[]{:S(2)}) copy-start(bf16[12,64,128]{2,1,0:T(8,128)(2,1)S(1)} %convolution_convert_fusion.7) | copy-start | bytes 589828
  131.4 128.3 %copy-start.29 = (f32[128,768]{1,0:T(8,128)}, f32[128,768]{1,0:T(8,128)S(1)}, u32[]{:S(2)}) copy-start(f32[128,768]{1,0:T(8,128)S(1)} %get-tuple-element.114) | copy-start | bytes 1179652
  131.4 66.8 %copy-start.186 = (f32[128]{0:T(128)}, f32[128]{0:T(128)S(1)}, u32[]{:S(2)}) copy-start(f32[128]{0:T(128)S(1)} %broadcast_multiply_fusion.6) | copy-start | bytes 1540
  131.6 66.6 %copy-start.228 = (f32[128]{0:T(128)}, f32[128]{0:T(128)S(1)}, u32[]{:S(2)}) copy-start(f32[128]{0:T(128)S(1)} %multiply_reduce_fusion.24) | copy-start | bytes 1540
  131.7 66.6 %copy-start.209 = (f32[128]{0:T(128)}, f32[128]{0:T(128)S(1)}, u32[]{:S(2)}) copy-start(f32[128]{0:T(128)S(1)} %fusion.129) | copy-start | bytes 1540
  132.3 127.4 %copy-start.215 = (f32[768]{0:T(1024)S(1)}, f32[768]{0:T(1024)}, u32[]{:S(2)}) copy-start(f32[768]{0:T(1024)} %convert_element_type.423) | copy-start | bytes 9220
  198.3 65.0 %copy-start.51 = (f32[128,3072]{1,0:T(8,128)}, f32[128,3072]{1,0:T(8,128)S(1)}, u32[]{:S(2)}) copy-start(f32[128,3072]{1,0:T(8,128)S(1)} %convolution_add_fusion.7) | copy-start | bytes 4718596
  263.4 5.1 slice-start
  269.5 5.4 copy-start.1
  269.5 5.4 copy-start.81
  269.5 5.4 copy-start.117
  269.5 5.4 copy-start.135
  286.3 5.6 copy-start.82
  286.3 5.6 copy-start.118
  286.3 5.6 copy-start.136
  299.6 11.9 %copy-start.21 = (f32[128,768]{1,0:T(8,128)}, f32[128,768]{1,0:T(8,128)S(1)}, u32[]{:S(2)}) copy-start(f32[128,768]{1,0:T(8,128)S(1)} %get-tuple-element.132) | copy-start | bytes 1179652
  299.7 11.9 %copy-start.153 = (f32[128]{0:T(128)}, f32[128]{0:T(128)S(1)}, u32[]{:S(2)}) copy-start(f32[128]{0:T(128)S(1)} %broadcast_multiply_fusion) | copy-start | bytes 1540
  299.9 11.6 %copy-start.197 = (f32[128]{0:T(128)}, f32[128]{0:T(128)S(1)}, u32[]{:S(2)}) copy-start(f32[128]{0:T(128)S(1)} %fusion.135) | copy-start | bytes 1540
  299.9 9.3 %slice-start.2 = ((s8[4718592]{0:T(1024)(128)(4,1)}), s8[4194304]{0:T(1024)(128)(4,1)S(1)}, s32[]{:S(2)}) async-start(s8[4718592]{0:T(1024)(128)(4,1)} %bitcast.341), calls=%async_computation.14 | async-start | bytes 8388608
  303.3 5.9 copy-start.43
  303.3 5.9 slice-start.3
  324.2 6.9 slice-start.4
  325.0 6.1 copy-start.120
  325.0 9.0 %copy-start.62 = (f32[128,768]{1,0:T(8,128)}, f32[128,768]{1,0:T(8,128)S(1)}, u32[]{:S(2)}) copy-start(f32[128,768]{1,0:T(8,128)S(1)} %get-tuple-element.57) | copy-start | bytes 1179652
  325.3 5.8 slice-start.5
  325.3 5.8 copy-start.27
  325.3 5.8 copy-start.91
  325.3 5.8 copy-start.148
  325.3 5.8 copy-start.192
  346.5 6.2 copy-start.60
  371.5 5.7 copy-start.70
  386.8 222.9 %reduce-scatter.5.cloned.1.call-start = ((), (), s32[]{:S(2)}) async-start(), calls=%async_computation.8 | async-start | bytes 7299072 | tf_op jit(solution)/shard_map/reduce_scatter | solution.py:306
  400.9 350.4 %reduce-scatter.11.cloned.1.call-start = ((), (), s32[]{:S(2)}) async-start(), calls=%async_computation.11 | async-start | bytes 9732096 | tf_op jit(solution)/shard_map/reduce_scatter | solution.py:317
  401.1 6.7 copy-start.50
  401.1 6.7 copy-start.121
  407.9 5.3 copy-start.44
  407.9 5.3 copy-start.103
  426.5 466.4 %reduce-scatter.9.cloned.1.call-start = ((), (), s32[]{:S(2)}) async-start(), calls=%async_computation.10 | async-start | bytes 9732096 | tf_op jit(solution)/shard_map/reduce_scatter | solution.py:315
  430.0 5.3 copy-start.22
  430.0 5.2 copy-start.74
  430.0 5.2 copy-start.154
  430.0 5.2 copy-start.198
  452.6 14.1 %copy-start.87 = (f32[768]{0:T(1024)S(1)}, f32[768]{0:T(1024)}, u32[]{:S(2)}) copy-start(f32[768]{0:T(1024)} %copy-done.80) | copy-start | bytes 9220
  452.6 14.1 %copy-start.163 = (f32[128]{0:T(128)S(1)}, f32[128]{0:T(128)}, u32[]{:S(2)}) copy-start(f32[128]{0:T(128)} %copy-done.161) | copy-start | bytes 1540
  469.5 48.1 %copy-start.12 = (f32[128,768]{1,0:T(8,128)S(1)}, f32[128,768]{1,0:T(8,128)}, u32[]{:S(2)}) copy-start(f32[128,768]{1,0:T(8,128)} %copy-done.8) | copy-start | bytes 1179652
  469.5 48.1 %copy-start.23 = (f32[128,768]{1,0:T(8,128)S(1)}, f32[128,768]{1,0:T(8,128)}, u32[]{:S(2)}) copy-start(f32[128,768]{1,0:T(8,128)} %copy-done.21) | copy-start | bytes 1179652
  469.5 48.1 %copy-start.45 = (f32[128,3072]{1,0:T(8,128)S(1)}, f32[128,3072]{1,0:T(8,128)}, u32[]{:S(2)}) copy-start(f32[128,3072]{1,0:T(8,128)} %copy-done.43) | copy-start | bytes 4718596
  469.5 48.1 %copy-start.218 = (f32[768]{0:T(1024)S(1)}, f32[768]{0:T(1024)}, u32[]{:S(2)}) copy-start(f32[768]{0:T(1024)} %convert_element_type.423) | copy-start | bytes 9220
  (196 other events, 437.9 us)
Sparse Core Ops, SparseCore 0:
  10.9 62.8 all-gather.4
  76.7 52.9 all-gather.6
  132.6 62.3 all-gather.8
  197.8 61.8 all-gather.10
  386.9 97.9 reduce-scatter.6
  491.1 118.5 reduce-scatter.4
  616.1 135.0 reduce-scatter.10
  757.7 135.1 reduce-scatter.8
where the time goes:
time: 904 us; the launch traced here: 900 us
  waiting for transfers between devices  558 us (62%)
  matrix products  168 us (19%)
  blocking collectives  83 us (9%)
  local copies, waits for them, and re-layouts  47.5 us (5%)
  other arithmetic  24.3 us (3%)
  between operations  19 us (2%)
    reduce_scatter x1, waiting for transfers between devices, body(): lax.psum_scatter(sum_fc_w, ('dp', 'fsdp'), scatter_dimension=0, tiled=True)  142 us
    reduce_scatter x1, waiting for transfers between devices, body(): lax.psum_scatter(sum_proj_w, ('dp', 'fsdp'), scatter_dimension=0, tiled=T...  142 us
    reduce_scatter x1, waiting for transfers between devices, body(): lax.psum_scatter(sum_qkv_w, ('dp', 'fsdp'), scatter_dimension=0, tiled=True)  87.8 us
    unnamed x2, blocking collectives  83 us
    all_gather x1, waiting for transfers between devices, fetch_mlp(): lax.all_gather(fc_weight, ('dp', 'fsdp'), axis=0, tiled=True)  62.8 us
    all_gather x1, waiting for transfers between devices, fetch_mlp(): lax.all_gather(proj_weight, ('dp', 'fsdp'), axis=0, tiled=True)  61.4 us
    all_gather x1, waiting for transfers between devices, fetch_attention(): lax.all_gather(out_weight, ('dp', 'fsdp'), axis=0, tiled=True)  51.2 us
    dot_general x4, matrix products, backward_mlp(): jnp.einsum('td,tf->df', normed_two, grad_upper, preferred_element_type=jn...  25.3 us
  transfers between devices with their start and end apart: 8, of which 7 were waited for; matrix products, arithmetic and copies ran while one was open for 12% of the time, Pallas kernels for 0%

commit v1 on v0

--- a/solution.py
+++ b/solution.py
@@ -8,6 +8,27 @@
 epsilon = 1e-05
 score_scale = 0.125
 gelu_coef = 0.7978845608028654
+
+
+def laid_out(parts, dim):
+    shape = list(parts.shape[1:])
+    shape[dim] *= parts.shape[0]
+    return jnp.moveaxis(parts, 0, dim).reshape(shape)
+
+
+def grow_blocks(value, axis):
+    size, here = (lax.axis_size(axis), lax.axis_index(axis))
+    pieces, bit = (value[None], 1)
+    while bit < size:
+        theirs = lax.ppermute(pieces, axis, [(i, i ^ bit) for i in range(size)])
+        low = here & bit == 0
+        pieces = jnp.concatenate([jnp.where(low, pieces, theirs), jnp.where(low, theirs, pieces)])
+        bit *= 2
+    return pieces
+
+
+def doubled_up(x, axis, dim):
+    return laid_out(grow_blocks(x, axis), dim)
 
 
 def layer_norm(values, gain, shift):
@@ -39,7 +60,7 @@
         lax.all_gather(ln2_bias, ("dp", "fsdp"), axis=0, tiled=True),
         lax.all_gather(fc_weight, ("dp", "fsdp"), axis=0, tiled=True),
         lax.all_gather(fc_bias, ("dp", "fsdp"), axis=0, tiled=True),
-        lax.all_gather(proj_weight, ("dp", "fsdp"), axis=0, tiled=True),
+        doubled_up(proj_weight, ("dp", "fsdp"), 0),
         lax.all_gather(proj_bias, ("dp", "fsdp"), axis=0, tiled=True),
     )
 

time: 904 us -> 867 us (0.959)
  waiting for transfers between devices: 558 us -> 455 us
  blocking collectives: 83 us -> 132 us
    all_gather x1 -> x0, waiting for transfers between devices: 61.4 us -> none  [fetch_mlp(): lax.all_gather(proj_weight, ('dp', 'fsdp'), axis=0, tiled=True)]
    all_gather x1, waiting for transfers between devices: 51.2 us -> 0.02 us  [fetch_attention(): lax.all_gather(out_weight, ('dp', 'fsdp'), axis=0, tiled=True)]
    unnamed x2, blocking collectives: 83 us -> 132 us
    ppermute x0 -> x5, waiting for transfers between devices: none -> 40.8 us  [grow_blocks(): theirs = lax.ppermute(pieces, axis, [(i, i ^ bit) for i in range(size)])]
    all_gather x1, waiting for transfers between devices: 62.8 us -> 41.6 us  [fetch_mlp(): lax.all_gather(fc_weight, ('dp', 'fsdp'), axis=0, tiled=True)]
    unnamed x528 -> x548, local copies, waits for them, and re-layouts: 22.4 us -> 18.9 us
  transfers between devices with their start and end apart: 8 -> 12, of which waited for: 7 -> 8; matrix products, arithmetic and copies ran while one was open for 12% -> 13% of each run, Pallas kernels for 0% -> 0%
where the time goes in v1:
time: 867 us; the launch traced here: 861 us
  waiting for transfers between devices  455 us (52%)
  matrix products  171 us (20%)
  blocking collectives  132 us (15%)
  local copies, waits for them, and re-layouts  44 us (5%)
  other arithmetic  30.3 us (3%)
  between operations  19.2 us (2%)
  starting transfers between devices  9.35 us (1%)
    reduce_scatter x1, waiting for transfers between devices, body(): lax.psum_scatter(sum_fc_w, ('dp', 'fsdp'), scatter_dimension=0, tiled=True)  142 us
    reduce_scatter x1, waiting for transfers between devices, body(): lax.psum_scatter(sum_proj_w, ('dp', 'fsdp'), scatter_dimension=0, tiled=T...  141 us
    unnamed x2, blocking collectives  132 us
    reduce_scatter x1, waiting for transfers between devices, body(): lax.psum_scatter(sum_qkv_w, ('dp', 'fsdp'), scatter_dimension=0, tiled=True)  87.6 us
    all_gather x1, waiting for transfers between devices, fetch_mlp(): lax.all_gather(fc_weight, ('dp', 'fsdp'), axis=0, tiled=True)  41.6 us
    ppermute x5, waiting for transfers between devices, grow_blocks(): theirs = lax.ppermute(pieces, axis, [(i, i ^ bit) for i in range(size)])  40.8 us
    dot_general x4, matrix products, backward_mlp(): jnp.einsum('td,tf->df', normed_two, grad_upper, preferred_element_type=jn...  25.4 us
    dot_general x4, matrix products, backward_mlp(): jnp.einsum('ti,to->io', activated, grad_branch, preferred_element_type=jn...  25.2 us
  transfers between devices with their start and end apart: 12, of which 8 were waited for; matrix products, arithmetic and copies ran while one was open for 13% of the time, Pallas kernels for 0%

profile of v1, /device:TPU:0, one launch (start us, length us, event | category | flops | bytes accessed | tf_op | source)
XLA Modules:
  0.0 861.3 jit_solution(3976342734191273495)
XLA Ops:
  9.4 3.1 collective-permute-start
  12.5 4.1 collective-permute-done
  17.5 1.9 collective-permute-start.1
  19.4 6.9 collective-permute-done.1
  26.4 2.9 collective-permute-start.2
  29.3 26.9 %collective-permute-done.2 = bf16[4,96,768]{2,1,0:T(8,128)(2,1)S(1)} collective-permute-done((bf16[4,96,768]{2,1,0:T(8,128)(2,1)S(1)}, bf16[4,96,768]{2,1,0:T(8,128)(2,1)S(1)}, u32[]{:S(2)}, u32[]{:S(2)}) %collective-permute-start.2) | collective-permute-done | bytes 589856 | tf_op jit(solution)/shard_map/ppermute | solution.py:23
  57.3 3.0 collective-permute-done.3
  60.3 1.6 broadcast_select_fusion.3
  62.0 1.6 pad_maximum_fusion.1
  67.8 91.9 %all-reduce.17 = (bf16[1536]{0:T(1024)(128)(2,1)S(1)}, bf16[768]{0:T(1024)(128)(2,1)S(1)}, bf16[768]{0:T(1024)(128)(2,1)S(1)}, bf16[768]{0:T(1024)(128)(2,1)S(1)...) all-reduce(bf16[1536]{0:T(1024)(128)(2,1)S(1)} %dynamic-update-slic, ...), channel_id=1, replica_groups=mesh['dp'=4,'fsdp'=8] {'dp','fsdp'}, use_global_device_ids=true, to_apply=%add.2 | all-reduce | flops 9216 | bytes 36864
  161.3 2.0 broadcast_select_fusion.1
  163.3 2.5 pad_maximum_fusion
  165.8 2.7 fusion
  170.4 1.8 fusion.180
  173.0 41.6 %all-gather.8.cloned.1.call-done = bf16[768,3072]{1,0:T(8,128)(2,1)} async-done(((bf16[24,3072]{1,0:T(8,128)(2,1)}), bf16[768,3072]{1,0:T(8,128)(2,1)}) %all-gather.8.cloned.1.call-update) | async-done | bytes 4718608 | tf_op jit(solution)/shard_map/all_gather | solution.py:61
  214.7 3.2 convolution_add_fusion.7
  217.9 4.1 fusion.181
  224.9 1.6 copy-done.2
  228.3 4.1 fusion.183
  235.2 2.2 copy.95
  241.7 3.2 convolution_add_fusion.5
  245.0 4.2 fusion.185
  252.1 2.1 copy.97
  258.6 3.3 convolution_add_fusion.4
  262.0 5.9 convert_reduce_fusion.3
  267.9 2.3 multiply_reduce_fusion.7
  273.8 1.7 copy.99
  275.6 1.6 convolution_bitcast_fusion.3
  280.6 2.0 multiply_reduce_fusion.10
  284.0 6.0 convert_reduce_fusion.2
  290.1 2.3 multiply_reduce_fusion.6
  295.3 1.7 copy.103
  297.1 1.6 convolution_bitcast_fusion.2
  302.1 2.0 multiply_reduce_fusion.9
  305.5 5.8 convert_reduce_fusion.1
  311.4 2.3 multiply_reduce_fusion.5
  316.6 1.7 copy.107
  318.3 1.6 convolution_bitcast_fusion.1
  322.5 1.9 fusion.189
  324.4 1.9 fusion.188
  326.4 1.9 fusion.187
  329.4 2.4 multiply_reduce_fusion.8
  333.2 3.0 convert_reduce_fusion
  336.2 2.3 multiply_reduce_fusion.4
  341.5 1.7 copy.111
  343.2 5.2 add_add_fusion.3
  348.5 1.8 multiply_reduce_fusion
  351.6 1.7 convert_reduce_fusion.4
  357.3 5.2 add_add_fusion.2
  362.8 6.7 fusion.157
  369.5 5.3 fusion.158
  374.8 1.6 fusion.126
  376.3 11.7 %add_add_fusion = f32[3072,768]{1,0:T(8,128)} fusion(f32[3072,768]{1,0:T(8,128)} %fusion.157, f32[3072,768]{1,0:T(8,128)S(1)} %fusion.126, f32[3072,768]{1,0:T(8,128)} %fusion.158, bf16[128,768]{1,0:T(8,128)(2,1)} %copy-done.124, f32[128,3072]{1,0:T(8,128)S(1)} %copy-done.53), kind=kOutput, calls=%fused_computation | convolution fusion | flops 614596608 | bytes 39518208 | tf_op jit(solution)/shard_map/ti,to->io/dot_general | solution.py:205
  388.7 2.8 fusion.152
  391.7 5.2 fusion.154
  396.9 5.1 fusion.156
  402.1 12.2 %add_add_fusion.1 = f32[768,3072]{1,0:T(8,128)} fusion(f32[768,3072]{1,0:T(8,128)S(1)} %fusion.152, f32[768,3072]{1,0:T(8,128)} %fusion.156, f32[768,3072]{1,0:T(8,128)} %fusion.154, bf16[128,3072]{1,0:T(8,128)(2,1)S(1)} %copy-done.80, f32[128,768]{1,0:T(8,128)S(1)} %copy-done.31, f32[768]{0:T(1024)S(1)} %copy-done.116, f32[768]{0:T(1024)S(1)} %copy-done.95, ...), kind=kOutput, calls=%fused_computation.1 | convolution fusion | flops 611549184 | bytes 38935552 | tf_op jit(solution)/shard_map/td,tf->df/dot_general | solution.py:212
  428.7 2.5 fusion.159
  432.3 40.0 %all-reduce.16 = (f32[768]{0:T(1024)S(1)}, f32[768]{0:T(1024)S(1)}, f32[1536]{0:T(1024)S(1)}, f32[768]{0:T(1024)S(1)}, f32[768]{0:T(1024)S(1)}, /*index=5*/f32[7...) all-reduce(f32[768]{0:T(1024)S(1)} %get-tuple-element.164, ...), channel_id=2, replica_groups=mesh['dp'=4,'fsdp'=8] {'dp','fsdp'}, use_global_device_ids=true, to_apply=%region_48.49.clone | all-reduce | flops 9216 | bytes 73728
  477.0 2.4 add_bitcast_fusion
  479.4 4.2 fusion.49
  483.6 87.6 %reduce-scatter.5.cloned.1.call-done = f32[24,2304]{1,0:T(8,128)} async-done(((f32[768,2304]{1,0:T(8,128)}), f32[24,2304]{1,0:T(8,128)}) %reduce-scatter.5.cloned.1.call-update) | async-done | bytes 221200 | tf_op jit(solution)/shard_map/reduce_scatter | solution.py:327
  571.2 141.5 %reduce-scatter.11.cloned.1.call-done = f32[96,768]{1,0:T(8,128)} async-done(((f32[3072,768]{1,0:T(8,128)}), f32[96,768]{1,0:T(8,128)}) %reduce-scatter.11.cloned.1.call-update) | async-done | bytes 294928 | tf_op jit(solution)/shard_map/reduce_scatter | solution.py:338
  712.7 141.6 %reduce-scatter.9.cloned.1.call-done = f32[24,3072]{1,0:T(8,128)} async-done(((f32[768,3072]{1,0:T(8,128)}), f32[24,3072]{1,0:T(8,128)}) %reduce-scatter.9.cloned.1.call-update) | async-done | bytes 294928 | tf_op jit(solution)/shard_map/reduce_scatter | solution.py:336
  (716 shorter events, 81.8 us)
Async XLA Ops:
  7.2 158.6 %all-gather.4.cloned.1.call-start = ((), (), s32[]{:S(2)}) async-start(), calls=%async_computation.4 | async-start | bytes 3649536 | tf_op jit(solution)/shard_map/all_gather | solution.py:50
  7.9 162.5 %all-gather.6.cloned.1.call-start = ((), (), s32[]{:S(2)}) async-start(), calls=%async_computation.5 | async-start | bytes 1216512 | tf_op jit(solution)/shard_map/all_gather | solution.py:52
  8.7 206.0 %all-gather.8.cloned.1.call-start = ((), (), s32[]{:S(2)}) async-start(), calls=%async_computation.6 | async-start | bytes 4866048 | tf_op jit(solution)/shard_map/all_gather | solution.py:61
  9.4 474.2 %reduce-scatter.7.cloned.1.call-start = ((), (), s32[]{:S(2)}) async-start(), calls=%async_computation.8 | async-start | bytes 2433024 | tf_op jit(solution)/shard_map/reduce_scatter | solution.py:329
  9.4 7.1 collective-permute-start
  17.5 8.7 %collective-permute-start.1 = (bf16[2,96,768]{2,1,0:T(8,128)(2,1)S(1)}, bf16[2,96,768]{2,1,0:T(8,128)(2,1)S(1)}, u32[]{:S(2)}, u32[]{:S(2)}) collective-permute-start(bf16[2,96,768]{2,1,0:T(8,128)(2,1)S(1)} %pad_maximum_fusion.4), channel_id=1, source_target_pairs={{0,2},{1,3},{2,0},{3,1},{4,6},{5,7},{6,4},{7,5},{8,10},{9,11},{10,... | collective-permute-start | bytes 884744 | tf_op jit(solution)/shard_map/ppermute | solution.py:23
  26.4 29.8 %collective-permute-start.2 = (bf16[4,96,768]{2,1,0:T(8,128)(2,1)S(1)}, bf16[4,96,768]{2,1,0:T(8,128)(2,1)S(1)}, u32[]{:S(2)}, u32[]{:S(2)}) collective-permute-start(bf16[4,96,768]{2,1,0:T(8,128)(2,1)S(1)} %pad_maximum_fusion.3), channel_id=1, source_target_pairs={{0,4},{1,5},{2,6},{3,7},{4,0},{5,1},{6,2},{7,3},{8,12},{9,13},{10,... | collective-permute-start | bytes 1769480 | tf_op jit(solution)/shard_map/ppermute | solution.py:23
  57.2 3.0 collective-permute-start.3
  61.9 5.6 copy-start.248
  61.9 98.5 %copy-start.32 = (bf16[1,128,768]{2,1,0:T(8,128)(2,1)S(1)}, bf16[1,128,768]{2,1,0:T(8,128)(2,1)}, u32[]{:S(2)}) copy-start(bf16[1,128,768]{2,1,0:T(8,128)(2,1)} %param.17) | copy-start | bytes 589828
  61.9 98.9 %copy-start.249 = (s32[1,128]{1,0:T(1,128)S(1)}, s32[1,128]{1,0:T(1,128)}, u32[]{:S(2)}) copy-start(s32[1,128]{1,0:T(1,128)} %param.20) | copy-start | bytes 1540
  63.5 97.8 %collective-permute-start.4 = (bf16[16,96,768]{2,1,0:T(8,128)(2,1)}, bf16[16,96,768]{2,1,0:T(8,128)(2,1)}, u32[]{:S(2)}, u32[]{:S(2)}) collective-permute-start(bf16[16,96,768]{2,1,0:T(8,128)(2,1)} %pad_maximum_fusion.1), channel_id=1, source_target_pairs={{0,16},{1,17},{2,18},{3,19},{4,20},{5,21},{6,22},{7,23},{8,24},{9,... | collective-permute-start | bytes 7077896 | tf_op jit(solution)/shard_map/ppermute | solution.py:23
  159.7 62.6 %copy-start.81 = (f32[768]{0:T(1024)}, f32[768]{0:T(1024)S(1)}, u32[]{:S(2)}) copy-start(f32[768]{0:T(1024)S(1)} %convert_element_type.413) | copy-start | bytes 9220
  159.7 67.4 %copy-start.89 = (f32[768]{0:T(1024)}, f32[768]{0:T(1024)S(1)}, u32[]{:S(2)}) copy-start(f32[768]{0:T(1024)S(1)} %convert_element_type.424) | copy-start | bytes 9220
  159.8 62.5 %copy-start.117 = (f32[768]{0:T(1024)}, f32[768]{0:T(1024)S(1)}, u32[]{:S(2)}) copy-start(f32[768]{0:T(1024)S(1)} %convert_element_type.414) | copy-start | bytes 9220
  159.8 67.4 %copy-start.113 = (f32[768]{0:T(1024)}, f32[768]{0:T(1024)S(1)}, u32[]{:S(2)}) copy-start(f32[768]{0:T(1024)S(1)} %convert_element_type.425) | copy-start | bytes 9220
  159.8 65.1 %copy-start.142 = (f32[768]{0:T(1024)}, f32[768]{0:T(1024)S(1)}, u32[]{:S(2)}) copy-start(f32[768]{0:T(1024)S(1)} %convert_element_type.423) | copy-start | bytes 9220
  160.4 66.8 %copy-start.132 = (f32[3072]{0:T(1024)}, f32[3072]{0:T(1024)S(1)}, u32[]{:S(2)}) copy-start(f32[3072]{0:T(1024)S(1)} %convert_element_type.427) | copy-start | bytes 36868
  160.4 61.9 %copy-start.135 = (f32[2304]{0:T(1024)}, f32[2304]{0:T(1024)S(1)}, u32[]{:S(2)}) copy-start(f32[2304]{0:T(1024)S(1)} %pad_maximum_fusion.5) | copy-start | bytes 27652
  170.4 47.5 %copy-start.125 = (bf16[12,64,128]{2,1,0:T(8,128)(2,1)}, bf16[12,64,128]{2,1,0:T(8,128)(2,1)S(1)}, u32[]{:S(2)}) copy-start(bf16[12,64,128]{2,1,0:T(8,128)(2,1)S(1)} %convolution_convert_fusion.7) | copy-start | bytes 589828
  172.2 45.7 %copy-start.29 = (f32[128,768]{1,0:T(8,128)}, f32[128,768]{1,0:T(8,128)S(1)}, u32[]{:S(2)}) copy-start(f32[128,768]{1,0:T(8,128)S(1)} %get-tuple-element.124) | copy-start | bytes 1179652
  172.2 45.7 %copy-start.187 = (f32[128]{0:T(128)}, f32[128]{0:T(128)S(1)}, u32[]{:S(2)}) copy-start(f32[128]{0:T(128)S(1)} %broadcast_multiply_fusion.6) | copy-start | bytes 1540
  172.4 45.5 %copy-start.229 = (f32[128]{0:T(128)}, f32[128]{0:T(128)S(1)}, u32[]{:S(2)}) copy-start(f32[128]{0:T(128)S(1)} %multiply_reduce_fusion.24) | copy-start | bytes 1540
  172.4 45.5 %copy-start.210 = (f32[128]{0:T(128)}, f32[128]{0:T(128)S(1)}, u32[]{:S(2)}) copy-start(f32[128]{0:T(128)S(1)} %fusion.133) | copy-start | bytes 1540
  173.0 44.9 %copy-start.216 = (f32[768]{0:T(1024)S(1)}, f32[768]{0:T(1024)}, u32[]{:S(2)}) copy-start(f32[768]{0:T(1024)} %convert_element_type.429) | copy-start | bytes 9220
  245.0 5.5 copy-start.83
  245.0 5.5 copy-start.119
  245.0 5.5 copy-start.137
  258.4 11.9 %copy-start.21 = (f32[128,768]{1,0:T(8,128)}, f32[128,768]{1,0:T(8,128)S(1)}, u32[]{:S(2)}) copy-start(f32[128,768]{1,0:T(8,128)S(1)} %get-tuple-element.142) | copy-start | bytes 1179652
  258.4 11.9 %copy-start.154 = (f32[128]{0:T(128)}, f32[128]{0:T(128)S(1)}, u32[]{:S(2)}) copy-start(f32[128]{0:T(128)S(1)} %broadcast_multiply_fusion) | copy-start | bytes 1540
  258.6 11.6 %copy-start.198 = (f32[128]{0:T(128)}, f32[128]{0:T(128)S(1)}, u32[]{:S(2)}) copy-start(f32[128]{0:T(128)S(1)} %fusion.139) | copy-start | bytes 1540
  258.6 9.3 %slice-start.2 = ((s8[4718592]{0:T(1024)(128)(4,1)}), s8[4194304]{0:T(1024)(128)(4,1)S(1)}, s32[]{:S(2)}) async-start(s8[4718592]{0:T(1024)(128)(4,1)} %bitcast.347), calls=%async_computation.13 | async-start | bytes 8388608
  262.0 5.9 copy-start.43
  262.0 5.9 slice-start.3
  282.9 7.1 slice-start.4
  283.7 6.3 copy-start.121
  283.7 9.0 %copy-start.63 = (f32[128,768]{1,0:T(8,128)}, f32[128,768]{1,0:T(8,128)S(1)}, u32[]{:S(2)}) copy-start(f32[128,768]{1,0:T(8,128)S(1)} %get-tuple-element.57) | copy-start | bytes 1179652
  284.0 6.0 slice-start.5
  284.0 6.0 copy-start.27
  284.0 6.0 copy-start.92
  284.0 6.1 copy-start.149
  284.0 6.1 copy-start.193
  304.1 7.2 slice-start.6
  305.1 6.2 copy-start.123
  305.1 8.8 %copy-start.61 = (f32[128,768]{1,0:T(8,128)}, f32[128,768]{1,0:T(8,128)S(1)}, u32[]{:S(2)}) copy-start(f32[128,768]{1,0:T(8,128)S(1)} %get-tuple-element.60) | copy-start | bytes 1179652
  305.5 5.8 slice-start.7
  305.5 5.8 copy-start.25
  305.5 5.8 copy-start.93
  305.5 5.8 copy-start.146
  305.5 5.8 copy-start.191
  321.5 11.4 %slice-start.10 = ((s8[4718592]{0:T(1024)(128)(4,1)}), s8[4194304]{0:T(1024)(128)(4,1)S(1)}, s32[]{:S(2)}) async-start(s8[4718592]{0:T(1024)(128)(4,1)} %bitcast.370), calls=%async_computation.21 | async-start | bytes 8388608
  326.4 6.5 slice-start.11
  332.9 6.0 copy-start.71
  348.4 222.8 %reduce-scatter.5.cloned.1.call-start = ((), (), s32[]{:S(2)}) async-start(), calls=%async_computation.7 | async-start | bytes 7299072 | tf_op jit(solution)/shard_map/reduce_scatter | solution.py:327
  362.5 350.2 %reduce-scatter.11.cloned.1.call-start = ((), (), s32[]{:S(2)}) async-start(), calls=%async_computation.10 | async-start | bytes 9732096 | tf_op jit(solution)/shard_map/reduce_scatter | solution.py:338
  362.8 6.7 copy-start.50
  362.8 6.7 copy-start.122
  388.1 466.2 %reduce-scatter.9.cloned.1.call-start = ((), (), s32[]{:S(2)}) async-start(), calls=%async_computation.9 | async-start | bytes 9732096 | tf_op jit(solution)/shard_map/reduce_scatter | solution.py:336
  414.3 14.1 %copy-start.88 = (f32[768]{0:T(1024)S(1)}, f32[768]{0:T(1024)}, u32[]{:S(2)}) copy-start(f32[768]{0:T(1024)} %copy-done.81) | copy-start | bytes 9220
  414.3 14.1 %copy-start.164 = (f32[128]{0:T(128)S(1)}, f32[128]{0:T(128)}, u32[]{:S(2)}) copy-start(f32[128]{0:T(128)} %copy-done.162) | copy-start | bytes 1540
  431.3 48.1 %copy-start.12 = (f32[128,768]{1,0:T(8,128)S(1)}, f32[128,768]{1,0:T(8,128)}, u32[]{:S(2)}) copy-start(f32[128,768]{1,0:T(8,128)} %copy-done.8) | copy-start | bytes 1179652
  431.3 48.1 %copy-start.23 = (f32[128,768]{1,0:T(8,128)S(1)}, f32[128,768]{1,0:T(8,128)}, u32[]{:S(2)}) copy-start(f32[128,768]{1,0:T(8,128)} %copy-done.21) | copy-start | bytes 1179652
  431.3 48.1 %copy-start.45 = (f32[128,3072]{1,0:T(8,128)S(1)}, f32[128,3072]{1,0:T(8,128)}, u32[]{:S(2)}) copy-start(f32[128,3072]{1,0:T(8,128)} %copy-done.43) | copy-start | bytes 4718596
  431.3 48.1 %copy-start.219 = (f32[768]{0:T(1024)S(1)}, f32[768]{0:T(1024)}, u32[]{:S(2)}) copy-start(f32[768]{0:T(1024)} %convert_element_type.429) | copy-start | bytes 9220
  (210 other events, 516.9 us)
Sparse Core Ops, SparseCore 0:
  10.9 81.5 all-gather.3
  95.4 53.6 all-gather.5
  152.0 62.5 all-gather.7
  348.6 97.8 reduce-scatter.6
  452.6 118.5 reduce-scatter.4
  577.5 135.1 reduce-scatter.10
  719.2 135.0 reduce-scatter.8
